TPU v7x, 32 devices: a whole 2x2x4 slice. The times are simulated.
32 devices in a mesh: tm: 8 (over z, x), space: 4 (over y, core).
Axes of the slice: x: 2, y: 2, z: 4, core: 2. Of those that a mesh axis runs over, the one named last changes fastest.
Arguments:
- frames: bfloat16 [32, 16, 128, 128], P('tm', 'space'), may hold values from -6 to 6
- conv_weight: bfloat16 [3456, 128], replicated, may hold values from -0.109375 to 0.109375
- conv_bias: float32 [128], replicated, may hold values from -3 to 3
- projection: float32 [128, 6], replicated, may hold values from -1 to 1
- levels: int32 [6], replicated, may hold values from 3 to 8, as said below
- centres: int32 [8, 16, 768], P(None, 'space', 'tm'), may hold values from 0 to 7, as said below
- code_grad: float32 [8, 16, 768], P(None, 'space', 'tm'), may hold values from -6 to 6
Outputs:
- quantized: float32 [8, 16, 768], P(None, 'space', 'tm')
- weight_grad: float32 [3456, 128], P('tm', 'space')
- projection_grad: float32 [128, 6], replicated
- bias_grad: float32 [128], replicated
Inputs may be any that keep to these rules, and one draw needn't show every extreme that they name: Level counts of the FSQ channels; in every draw some channel has 3 levels and some has 8. centres[g, h, q] is below levels[q % 6].
All inputs are finite; a program needn't handle non-finite values.
Results may differ from a plain program's by a relative error of at most 0.0024.
Values may be sent and summed in bfloat16 or wider, within the bound.
A program may use at most 64 MiB of HBM per device.

v0:
```python
import functools

import jax
import jax.numpy as jnp
from jax import lax
from jax.experimental import pallas as pl
from jax.experimental.pallas import tpu as pltpu
from jax.sharding import PartitionSpec as P

offset_scale = 0.45
commit_weight = 0.25
highest = lax.Precision.HIGHEST
MESH = pl.DeviceIdType.MESH
f32, bf16 = jnp.float32, jnp.bfloat16
core_type, row_type, time_type = f32, bf16, bf16


def dot(a, b, ca, cb, precision=None):
    return lax.dot_general(
        a, b, (((ca,), (cb,)), ((), ())), preferred_element_type=f32, precision=precision
    )


def per_level(levels_ref, index, count):
    half = jnp.ones(index.shape, f32)
    for j in range(count):
        half = jnp.where(index == j, (levels_ref[j].astype(f32) - 1.0) * 0.5, half)
    return half


def block_kernel(
    T, S, scale,
    frames, weight, bias, proj, levels, code_grad,
    weight_out, small_out,
    xb, cg_send, cg_recv, pscr, slope_t, gt, acc, stage1, recv1, sum2, stage2, recv2,
    total, own3, stage3, recv3, sm_send, sm_recv, st_send, st_recv,
    local_sem, halo_s, halo_r, cg_s, cg_r, ss_s, ss_r, ts_s, ts_r,
    core_s, core_r, y_s, y_r, tm_s, tm_r,
):
    Y = S // 2
    F, R, W, C = frames.shape
    L = levels.shape[0]
    TILE = code_grad.shape[2]
    oc = C // S
    KC = weight.shape[0]
    KA = KC // 3
    KT = KC // T
    KTP = stage3.shape[2]
    cells = R * W
    t = lax.axis_index("tm")
    s = lax.axis_index("space")
    y, core = s // 2, s % 2
    up_t, dn_t, up_s, dn_s = t < T - 1, t > 0, s < S - 1, s > 0

    barrier = pltpu.get_barrier_semaphore()

    def signal(tt, ss):
        pl.semaphore_signal(barrier, inc=1, device_id=(tt, ss), device_id_type=MESH)

    for d in range(1, S):
        signal(t, lax.rem(s + d, S))
    for d in range(1, T):
        signal(lax.rem(t + d, T), s)
    for ct, dt in ((up_t, 1), (dn_t, -1)):
        for cs_, ds in ((up_s, 1), (dn_s, -1)):
            @pl.when(jnp.logical_and(ct, cs_))
            def _():
                signal(t + dt, s + ds)

    own = pltpu.make_async_copy(frames, xb.at[2 : 2 + F, 1 : 1 + R], local_sem.at[0])
    own.start()
    first = [
        pltpu.make_async_copy(frames.at[0], xb.at[k, 1 : 1 + R], local_sem.at[1 + k])
        for k in range(2)
    ]

    @pl.when(t == 0)
    def _():
        for copy in first:
            copy.start()

    cg_send[...] = jnp.zeros_like(cg_send)
    cg_send[:, 0:R, 0:TILE] = code_grad[...]

    n_t = jnp.where(up_t, 1, 0) + jnp.where(dn_t, 1, 0)
    n_s = jnp.where(up_s, 1, 0) + jnp.where(dn_s, 1, 0)
    pl.semaphore_wait(barrier, (S - 1) + (T - 1) + n_t * n_s)

    def remote(src, dst, ss_, rs_, tt, sp):
        return pltpu.make_async_remote_copy(
            src_ref=src, dst_ref=dst, send_sem=ss_, recv_sem=rs_,
            device_id=(tt, sp), device_id_type=MESH,
        )

    H = R + 1
    halos = [
        (up_s, dn_s, remote(frames.at[:, R - 1], xb.at[2 : 2 + F, 0],
                            halo_s.at[0], halo_r.at[0], t, s + 1)),
        (dn_s, up_s, remote(frames.at[:, 0], xb.at[2 : 2 + F, H],
                            halo_s.at[1], halo_r.at[1], t, s - 1)),
        (up_t, dn_t, remote(frames.at[F - 2 : F], xb.at[0:2, 1:H],
                            halo_s.at[2], halo_r.at[2], t + 1, s)),
        (jnp.logical_and(up_t, up_s), jnp.logical_and(dn_t, dn_s),
         remote(frames.at[F - 2 : F, R - 1], xb.at[0:2, 0],
                halo_s.at[3], halo_r.at[3], t + 1, s + 1)),
        (jnp.logical_and(up_t, dn_s), jnp.logical_and(dn_t, up_s),
         remote(frames.at[F - 2 : F, 0], xb.at[0:2, H],
                halo_s.at[4], halo_r.at[4], t + 1, s - 1)),
    ]

    def start_if(cond, copy):
        @pl.when(cond)
        def _():
            copy.start()

    def recv_if(cond, copy):
        @pl.when(cond)
        def _():
            copy.wait_recv()

    def sent_if(cond, copy):
        @pl.when(cond)
        def _():
            copy.wait_send()

    for sends, _, copy in halos:
        start_if(sends, copy)

    def cg_copy(d):
        to = lax.rem(t + d, T)
        return remote(cg_send.at[to], cg_recv.at[d], cg_s.at[d], cg_r.at[d], to, s)

    for d in range(1, T):
        cg_copy(d).start()

    pscr[...] = jnp.zeros_like(pscr)
    pscr[0:L] = proj[...]
    proj_t = pscr[...]

    @pl.when(s == 0)
    def _():
        xb[:, 0] = jnp.zeros((F + 2, W, C), bf16)

    @pl.when(s == S - 1)
    def _():
        xb[:, H] = jnp.zeros((F + 2, W, C), bf16)

    row = lax.broadcasted_iota(jnp.int32, (cells, C), 0) % W

    def conv_frame(f):
        slabs = []
        weights = []
        for a in range(3):
            for b in range(3):
                slabs.append(xb[f + a, b : b + R].reshape(cells, C))
                k0 = (a * 3 + b) * 3 * C
                weights.append(
                    jnp.concatenate([weight[k0 + c * C : k0 + (c + 1) * C] for c in range(3)], 1)
                )
        out = dot(jnp.concatenate(slabs, 1), jnp.concatenate(weights, 0), 1, 0)
        left = jnp.where(row == 0, 0.0, pltpu.roll(out[:, 0:C], 1, 0))
        right = jnp.where(row == W - 1, 0.0, pltpu.roll(out[:, 2 * C :], cells - 1, 0))
        pre = out[:, C : 2 * C] + bias[...] + left + right
        sig = 1.0 / (1.0 + jnp.exp(-pre))
        act = (pre * sig).astype(bf16).astype(f32)
        slope = sig * (1.0 + pre * (1.0 - sig))
        for h in range(R):
            slope_t[f * R + h] = slope[h * W : (h + 1) * W].T
        return act

    own.wait()
    for _, gets, copy in halos[:2]:
        recv_if(gets, copy)
    pooled = conv_frame(2) + conv_frame(3)

    for _, gets, copy in halos[2:]:
        recv_if(gets, copy)

    @pl.when(t == 0)
    def _():
        for k in range(2):
            first[k].wait()
            xb[k, 0] = xb[2, 0]
            xb[k, H] = xb[2, H]

    pooled = (pooled + conv_frame(0) + conv_frame(1)) * 0.25

    for d in range(1, T):
        cg_copy(d).wait_recv()
    wt = TILE // L
    mine = cg_send[pl.ds(t, 1)]
    pieces = [mine]
    for d in range(1, T):
        pieces.append(cg_recv[d : d + 1])
    cg_all = jnp.concatenate(pieces, 0).reshape(T * 8, 128)
    r_i = lax.broadcasted_iota(jnp.int32, (T * 8, cells), 0)
    q_i = lax.broadcasted_iota(jnp.int32, (T * 8, cells), 1)
    owner = lax.rem(t - r_i // 8 + T, T)
    pick = jnp.logical_and(r_i % 8 == q_i // W, owner == (q_i % W) // wt).astype(f32)
    spread = dot(cg_all, pick, 0, 0, highest)
    l_i = lax.broadcasted_iota(jnp.int32, (128, cells), 0)
    w_i = lax.broadcasted_iota(jnp.int32, (128, cells), 1) % W
    spread = jnp.where(jnp.logical_and(l_i // L == w_i % wt, l_i < TILE), spread, 0.0)
    j_i = lax.broadcasted_iota(jnp.int32, (8, 128), 0)
    m_i = lax.broadcasted_iota(jnp.int32, (8, 128), 1)
    fold = jnp.logical_and(m_i % L == j_i, m_i < TILE).astype(f32)
    code = dot(fold, spread, 1, 0, highest)

    latent = dot(proj_t, pooled, 1, 1, highest)
    squashed = jnp.tanh(latent)
    half_j = per_level(levels, lax.broadcasted_iota(jnp.int32, (8, cells), 0), L)
    step = (
        (code / half_j + 2.0 * commit_weight * offset_scale * squashed)
        * offset_scale
        * (1.0 - squashed * squashed)
        * scale
    )
    proj_part = dot(step, pooled, 1, 0, highest)
    pg_t = dot(proj_t, step, 0, 0, highest) * 0.25

    lane = lax.broadcasted_iota(jnp.int32, (C, W), 1)
    bias_sum = jnp.zeros((C, W), f32)
    for f in range(F):
        for h in range(R):
            g = pg_t[:, h * W : (h + 1) * W] * slope_t[f * R + h]
            bias_sum = bias_sum + g
            q0 = (f * R + h) * W
            gt[0:C, q0 : q0 + W] = jnp.where(lane == W - 1, 0.0, pltpu.roll(g, W - 1, 1)).astype(bf16)
            gt[C : 2 * C, q0 : q0 + W] = g.astype(bf16)
            gt[2 * C :, q0 : q0 + W] = jnp.where(lane == 0, 0.0, pltpu.roll(g, 1, 1)).astype(bf16)
    bias_part = dot(jnp.ones((8, W), f32), bias_sum, 1, 1, highest)
    sm_send[...] = jnp.where(lax.broadcasted_iota(jnp.int32, (8, C), 0) == L, bias_part, proj_part)

    def small_space(d):
        return remote(sm_send, sm_recv.at[d], ss_s.at[d], ss_r.at[d], t, lax.rem(s + d, S))

    def small_time(d):
        return remote(st_send, st_recv.at[d], ts_s.at[d], ts_r.at[d], lax.rem(t + d, T), s)

    for d in range(1, S):
        small_space(d).start()

    def core_copy(a):
        return remote(stage1.at[a, 1 - core], recv1.at[a], core_s.at[a], core_r.at[a], t, s + 1 - 2 * core)

    def y_copy(a, d):
        to = lax.rem(y + d, Y)
        return remote(stage2.at[a, to], recv2.at[a, d], y_s.at[a, d], y_r.at[a, d], t, to * 2 + core)

    def tm_copy(to, slot):
        return remote(stage3.at[to], recv3.at[slot], tm_s.at[to], tm_r.at[slot], to, s)

    def products(a):
        rhs = jnp.concatenate(
            [xb[a : a + F, b : b + R].reshape(F * cells, C) for b in range(3)], 1
        )
        res = dot(gt[...], rhs, 1, 0)
        for b in range(3):
            for c in range(3):
                k0 = (b * 3 + c) * C
                for sp in range(S):
                    blk = res[c * C + sp * oc : c * C + (sp + 1) * oc, b * C : (b + 1) * C]
                    acc[a, sp % 2, sp // 2, :, k0 : k0 + C] = blk
                    stage1[a, sp % 2, sp // 2, :, k0 : k0 + C] = blk.astype(core_type)
        core_copy(a).start()

    def fold_core(a):
        core_copy(a).wait_recv()
        for yy in range(Y):
            v = acc[a, core, yy] + recv1[a, yy].astype(f32)
            sum2[a, yy] = v
            stage2[a, yy] = v.astype(row_type)
        for d in range(1, Y):
            y_copy(a, d).start()

    done = [0]

    def fold_y(a):
        v = sum2[a, y]
        for d in range(1, Y):
            y_copy(a, d).wait_recv()
            v = v + recv2[a, d].astype(f32)
        total[:, a * KA : (a + 1) * KA] = v
        while (done[0] + 1) * KT <= (a + 1) * KA:
            to = done[0]
            off = to * KT
            base = off // 128 * 128
            win = total[:, base : base + KTP + 128]
            if off > base:
                win = pltpu.roll(win, KTP + 128 - (off - base), 1)
            win = win[:, 0:KTP]
            own3[to] = win
            stage3[to] = win.astype(time_type)
            start_if(t != to, tm_copy(to, t))
            done[0] += 1

    total[:, KC:] = jnp.zeros((oc, total.shape[1] - KC), f32)
    products(0)
    sm = sm_send[...]
    for d in range(1, S):
        small_space(d).wait_recv()
        sm = sm + sm_recv[d]
    st_send[...] = sm
    for d in range(1, T):
        small_time(d).start()
    products(1)
    fold_core(0)
    products(2)
    fold_core(1)
    fold_y(0)
    fold_core(2)
    fold_y(1)
    fold_y(2)

    for d in range(1, T):
        small_time(d).wait_recv()
        sm = sm + st_recv[d]
    small_out[...] = sm

    res = own3[t]
    for d in range(1, T):
        src = lax.rem(t + d, T)
        tm_copy(src, src).wait_recv()
        res = res + recv3[src].astype(f32)
    weight_out[...] = res[:, 0:KT]

    for sends, _, copy in halos:
        sent_if(sends, copy)
    for d in range(1, T):
        cg_copy(d).wait_send()
        small_time(d).wait_send()
    for d in range(1, S):
        small_space(d).wait_send()
    for a in range(3):
        core_copy(a).wait_send()
        for d in range(1, Y):
            y_copy(a, d).wait_send()
    for to in range(T):
        sent_if(t != to, tm_copy(to, t))


def finish_kernel(levels, centres, wg, small, quant_out, weight_out, proj_out, bias_out):
    L = levels.shape[0]
    lane = lax.broadcasted_iota(jnp.int32, centres.shape, 2)
    half = per_level(levels, lax.rem(lane, L), L)
    quant_out[...] = (centres[...].astype(f32) - half) / half
    weight_out[...] = wg[...]
    proj_out[...] = small[0:L]
    bias_out[...] = small[L : L + 1]


def on_device(T, S, frames, conv_weight, conv_bias, projection, levels, centres, code_grad):
    F, R, W, C = frames.shape
    KC = conv_weight.shape[0]
    KT = KC // T
    KTP = -(-KT // 128) * 128
    oc, Y, cells = C // S, S // 2, R * W
    scale = float(F * T * R * S * W) ** -0.5
    vmem = pl.BlockSpec(memory_space=pltpu.VMEM)
    dma = pltpu.SemaphoreType.DMA
    KA = KC // 3
    wg, small = pl.pallas_call(
        functools.partial(block_kernel, T, S, scale),
        out_shape=(
            jax.ShapeDtypeStruct((oc, KT), f32),
            jax.ShapeDtypeStruct((8, C), f32),
        ),
        in_specs=[
            pl.BlockSpec(memory_space=pl.ANY), vmem, vmem, vmem,
            pl.BlockSpec(memory_space=pltpu.SMEM), vmem,
        ],
        out_specs=(vmem, vmem),
        scratch_shapes=[
            pltpu.VMEM((F + 2, R + 2, W, C), bf16),
            pltpu.VMEM((T, 8, 128), f32),
            pltpu.VMEM((T, 8, 128), f32),
            pltpu.VMEM((8, C), f32),
            pltpu.VMEM((F * R, C, W), f32),
            pltpu.VMEM((3 * C, F * cells), bf16),
            pltpu.VMEM((3, 2, Y, oc, KA), f32),
            pltpu.VMEM((3, 2, Y, oc, KA), core_type),
            pltpu.VMEM((3, Y, oc, KA), core_type),
            pltpu.VMEM((3, Y, oc, KA), f32),
            pltpu.VMEM((3, Y, oc, KA), row_type),
            pltpu.VMEM((3, Y, oc, KA), row_type),
            pltpu.VMEM((oc, KC + KTP + 128), f32),
            pltpu.VMEM((T, oc, KTP), f32),
            pltpu.VMEM((T, oc, KTP), time_type),
            pltpu.VMEM((T, oc, KTP), time_type),
            pltpu.VMEM((8, C), f32),
            pltpu.VMEM((S, 8, C), f32),
            pltpu.VMEM((8, C), f32),
            pltpu.VMEM((T, 8, C), f32),
            dma((3,)), dma((5,)), dma((5,)), dma((T,)), dma((T,)),
            dma((S,)), dma((S,)), dma((T,)), dma((T,)),
            dma((3,)), dma((3,)), dma((3, Y)), dma((3, Y)), dma((T,)), dma((T,)),
        ],
        compiler_params=pltpu.CompilerParams(
            collective_id=0, has_side_effects=True, vmem_limit_bytes=56 * 1024 * 1024
        ),
    )(frames, conv_weight, conv_bias.reshape(1, C), projection.T, levels, code_grad)
    L = levels.shape[0]
    quantized, wg, proj_grad, bias_grad = pl.pallas_call(
        finish_kernel,
        out_shape=(
            jax.ShapeDtypeStruct(centres.shape, f32),
            jax.ShapeDtypeStruct(wg.shape, f32),
            jax.ShapeDtypeStruct((L, C), f32),
            jax.ShapeDtypeStruct((1, C), f32),
        ),
        in_specs=[pl.BlockSpec(memory_space=pltpu.SMEM), vmem, vmem, vmem],
        out_specs=(vmem,) * 4,
    )(levels, centres, wg, small)
    return quantized, wg.T, proj_grad.T, bias_grad.reshape(C)


def solution(mesh):
    return jax.shard_map(
        functools.partial(on_device, mesh.shape["tm"], mesh.shape["space"]),
        mesh=mesh,
        in_specs=(
            P("tm", "space", None, None),
            P(),
            P(),
            P(),
            P(),
            P(None, "space", "tm"),
            P(None, "space", "tm"),
        ),
        out_specs=(P(None, "space", "tm"), P("tm", "space"), P(), P()),
        check_vma=False,
    )
```

profile of v0, /device:TPU:24, one launch (start us, length us, event | category | flops | bytes accessed | tf_op | source)
XLA Modules:
  0.0 38.0 jit_solution(15323667700094521630)
XLA Ops:
  0.6 35.8 %shard_map.102 = (f32[32,432]{1,0:T(8,128)}, f32[8,128]{1,0:T(8,128)}) custom-call(bf16[4,4,128,128]{3,2,1,0:T(8,128)(2,1)} %frames.1, bf16[3456,128]{1,0:T(8,128)(2,1)} %weight.1, f32[1,128]{1,0:T(1,128)} %bitcast.6, f32[6,128]{1,0:T(8,128)} %bitcast.5, s32[6]{0:T(128)} %levels.3, f32[8,4,96]{2,1,0:T(4,128)} %code_grad.1), custom_call_target="tpu_custom_call" | custom-call | tf_op jit(solution)/shard_map/pallas_call | solution.py:362
  36.5 1.5 %shard_map.103 = (f32[8,4,96]{2,1,0:T(4,128)}, f32[32,432]{1,0:T(8,128)}, f32[6,128]{1,0:T(8,128)}, f32[1,128]{1,0:T(1,128)}) custom-call(s32[6]{0:T(128)} %levels.3, s32[8,4,96]{2,1,0:T(4,128)} %centres.1, f32[32,432]{1,0:T(8,128)} %get-tuple-element.10.wg, f32[8,128]{1,0:T(8,128)} %get-tuple-element.11.small), custom_call_target="tpu_custom_call" | custom-call | tf_op jit(solution)/shard_map/pallas_call | solution.py:403
where the time goes:
time: 38.2 us; the launch traced here: 38 us
  Pallas kernels  37.3 us (98%)
  between operations  0.64 us (2%)
    pallas_call x1, Pallas kernels, on_device(): pl.pallas_call(functools.partial(block_kernel, T, S, scale), out_shape=(j...  35.8 us
    pallas_call x1, Pallas kernels, on_device(): pl.pallas_call(finish_kernel, out_shape=(jax.ShapeDtypeStruct(centres.sha...  1.5 us

commit v1 on v0

v1 whole, which is shorter than its diff:
```python
import functools

import jax
import jax.numpy as jnp
from jax import lax
from jax.experimental import pallas as pl
from jax.experimental.pallas import tpu as pltpu
from jax.sharding import PartitionSpec as P

offset_scale = 0.45
commit_weight = 0.25
highest = lax.Precision.HIGHEST
MESH = pl.DeviceIdType.MESH
f32, bf16 = jnp.float32, jnp.bfloat16
link_type = bf16


def dot(a, b, ca, cb, precision=None):
    return lax.dot_general(
        a, b, (((ca,), (cb,)), ((), ())), preferred_element_type=f32, precision=precision
    )


def per_level(levels_ref, index, count):
    half = jnp.ones(index.shape, f32)
    for j in range(count):
        half = jnp.where(index == j, (levels_ref[j].astype(f32) - 1.0) * 0.5, half)
    return half


def grid_of(T):
    X = max(d for d in range(1, T + 1) if T % d == 0 and d * d <= T)
    return T // X, X


def packed_rows(oc, KT):
    full, rest = KT // 128, KT % 128
    folded = 0 < rest <= 64 and oc % 32 == 0
    return full, rest, folded, full * oc + (oc // 2 if folded else oc if rest else 0)


def block_kernel(
    T, S, scale,
    frames, weight_in, bias_in, proj_in, levels_in, code_in,
    weight_out, small_out,
    xb, weight, bias, proj, levels, code_grad, cg_a, cg_b, cg_c, pscr, part, slope_t, gt, acc, recv1,
    sum2, stage2, recv2, own3, stage3, recv3,
    sm_send, sm_recv, sx_send, sx_recv, sz_send, sz_recv,
    local_sem, token, halo_s, halo_r, cx_s, cx_r, cz_s, cz_r, ss_s, ss_r, sx_s, sx_r, sz_s, sz_r,
    core_s, core_r, y_s, y_r, tm_s, tm_r,
):
    Y = S // 2
    Z, X = grid_of(T)
    F, R, W, C = frames.shape
    L = levels_in.shape[0]
    TILE = code_in.shape[2]
    oc = C // S
    KC = weight_in.shape[0]
    KT = KC // T
    KZ = KT * X
    G = 3 * C
    full, rest, folded, PB = packed_rows(oc, KT)
    cells = R * W
    t = lax.axis_index("tm")
    s = lax.axis_index("space")
    y, core = s // 2, s % 2
    z, x = t // X, t % X
    up_t, dn_t, up_s, dn_s = t < T - 1, t > 0, s < S - 1, s > 0
    up_z, dn_z = z < Z - 1, z > 0
    turn_up = jnp.logical_and(up_t, x == X - 1)
    turn_dn = jnp.logical_and(dn_t, x == 0)

    barrier = pltpu.get_barrier_semaphore()

    def signal(tt, ss, sem=barrier):
        pl.semaphore_signal(sem, inc=1, device_id=(tt, ss), device_id_type=MESH)

    def signal_if(cond, tt, ss, sem=barrier):
        @pl.when(cond)
        def _():
            signal(tt, ss, sem)

    signal_if(turn_up, t + 1, s)
    signal_if(turn_dn, t - 1, s)
    for dx in range(1, X):
        signal(z * X + lax.rem(x + dx, X), s)
    signal_if(up_z, t + X, s)
    signal_if(dn_z, t - X, s)
    for dy in range(1, Y):
        for dx in range(1, X):
            signal(z * X + lax.rem(x + dx, X), lax.rem(y + dy, Y) * 2 + core)
    for d in range(1, S):
        signal(t, lax.rem(s + d, S))

    own = pltpu.make_async_copy(frames, xb.at[2 : 2 + F, 1 : 1 + R], local_sem.at[0])
    first = [
        pltpu.make_async_copy(frames.at[0], xb.at[k, 1 : 1 + R], local_sem.at[1 + k])
        for k in range(2)
    ]
    code_load = pltpu.make_async_copy(code_in, code_grad, local_sem.at[3])
    proj_load = pltpu.make_async_copy(proj_in, proj, local_sem.at[4])
    bias_load = pltpu.make_async_copy(bias_in, bias, local_sem.at[5])
    levels_load = pltpu.make_async_copy(levels_in, levels, local_sem.at[6])
    weight_load = pltpu.make_async_copy(weight_in, weight, local_sem.at[7])
    code_load.start()
    own.start()
    weight_load.start()
    proj_load.start()
    bias_load.start()
    levels_load.start()

    @pl.when(t == 0)
    def _():
        for copy in first:
            copy.start()

    cg_a[...] = jnp.zeros_like(cg_a)
    pscr[...] = jnp.zeros_like(pscr)

    @pl.when(s == 0)
    def _():
        xb[:, 0] = jnp.zeros((F + 2, W, C), bf16)

    @pl.when(s == S - 1)
    def _():
        xb[:, R + 1] = jnp.zeros((F + 2, W, C), bf16)

    code_load.wait()
    for k in range(T):
        cg_a[k // X, k % X, 0:R, 0:TILE] = code_grad[k]
    cg_b[0] = cg_a[:, x]

    one = lambda c: jnp.where(c, 1, 0)
    pl.semaphore_wait(
        barrier,
        (S - 1) + (X - 1) * Y + one(up_z) + one(dn_z) + one(turn_up) + one(turn_dn),
    )

    def remote(src, dst, ss_, rs_, tt, sp):
        return pltpu.make_async_remote_copy(
            src_ref=src, dst_ref=dst, send_sem=ss_, recv_sem=rs_,
            device_id=(tt, sp), device_id_type=MESH,
        )

    def start_if(cond, copy):
        @pl.when(cond)
        def _():
            copy.start()

    def recv_if(cond, copy):
        @pl.when(cond)
        def _():
            copy.wait_recv()

    def sent_if(cond, copy):
        @pl.when(cond)
        def _():
            copy.wait_send()

    def cgx_copy(d):
        to = lax.rem(x + d, X)
        return remote(cg_a.at[:, to], cg_b.at[d], cx_s.at[d], cx_r.at[d], z * X + to, s)

    def cgz_copy(d):
        to = lax.rem(z + d, Z)
        return remote(cg_b.at[:, to], cg_c.at[d], cz_s.at[d], cz_r.at[d], to * X + x, s)

    H = R + 1

    def halo(k, src, dst, tt, sp):
        return remote(src, dst, halo_s.at[k], halo_r.at[k], tt, sp)

    row_up = halo(0, frames.at[:, R - 1], xb.at[2 : 2 + F, 0], t, s + 1)
    row_dn = halo(1, frames.at[:, 0], xb.at[2 : 2 + F, H], t, s - 1)
    edge_lo = halo(2, frames.at[F - 2 : F, 0], xb.at[0:2, 1], t + 1, s)
    edge_hi = halo(3, frames.at[F - 2 : F, R - 1], xb.at[0:2, R], t + 1, s)
    inner = halo(4, frames.at[F - 2 : F, 1 : R - 1], xb.at[0:2, 2:R], t + 1, s)
    pass_dn = halo(5, xb.at[0:2, 1], xb.at[0:2, H], t, s - 1)
    pass_up = halo(6, xb.at[0:2, R], xb.at[0:2, 0], t, s + 1)
    late_dn, late_up = jnp.logical_and(dn_t, dn_s), jnp.logical_and(dn_t, up_s)

    for d in range(1, X):
        cgx_copy(d).start()
    start_if(up_t, edge_lo)
    start_if(up_t, edge_hi)
    start_if(up_s, row_up)
    start_if(dn_s, row_dn)

    def token_send(r):
        signal_if(up_z, t + X, s, token.at[r, 0])
        signal_if(dn_z, t - X, s, token.at[r, 1])

    def token_wait(r):
        @pl.when(dn_z)
        def _():
            pl.semaphore_wait(token.at[r, 0], 1)

        @pl.when(up_z)
        def _():
            pl.semaphore_wait(token.at[r, 1], 1)

    for r in range(max(Z - 2, 0)):
        token_send(r)
        token_wait(r)
    for d in range(1, X):
        cgx_copy(d).wait_recv()
    for d in range(1, Z):
        cgz_copy(d).start()
    start_if(up_t, inner)

    proj_load.wait()
    bias_load.wait()
    levels_load.wait()
    pscr[0:L] = proj[...]
    proj_t = pscr[...]
    row = lax.broadcasted_iota(jnp.int32, (cells, C), 0) % W

    def taps(f, times):
        slabs = []
        weights = []
        for a in times:
            for b in range(3):
                slabs.append(xb[f + a, b : b + R].reshape(cells, C))
                k0 = (a * 3 + b) * G
                weights.append(
                    jnp.concatenate([weight[k0 + c * C : k0 + (c + 1) * C] for c in range(3)], 1)
                )
        return dot(jnp.concatenate(slabs, 1), jnp.concatenate(weights, 0), 1, 0)

    def frame_end(f, out):
        left = jnp.where(row == 0, 0.0, pltpu.roll(out[:, 0:C], 1, 0))
        right = jnp.where(row == W - 1, 0.0, pltpu.roll(out[:, 2 * C :], cells - 1, 0))
        pre = out[:, C : 2 * C] + bias[...] + left + right
        sig = 1.0 / (1.0 + jnp.exp(-pre))
        act = (pre * sig).astype(bf16).astype(f32)
        slope = sig * (1.0 + pre * (1.0 - sig))
        for h in range(R):
            slope_t[f * R + h] = slope[h * W : (h + 1) * W].T
        return act

    own.wait()
    weight_load.wait()
    recv_if(dn_s, row_up)
    recv_if(up_s, row_dn)
    pooled = frame_end(2, taps(2, (0, 1, 2)))

    recv_if(dn_t, edge_lo)
    start_if(late_dn, pass_dn)
    recv_if(dn_t, edge_hi)
    start_if(late_up, pass_up)
    pooled = pooled + frame_end(3, taps(3, (0, 1, 2)))
    part[0] = taps(0, (2,))
    part[1] = taps(1, (1, 2))

    cg_c[0] = cg_b[:, z]
    for d in range(1, Z):
        cgz_copy(d).wait_recv()
    wt = TILE // L
    cg_all = cg_c[...].reshape(T * 8, 128)
    r_i = lax.broadcasted_iota(jnp.int32, (T * 8, cells), 0)
    q_i = lax.broadcasted_iota(jnp.int32, (T * 8, cells), 1)
    piece = r_i // 8
    owner = lax.rem(z - piece // X + Z, Z) * X + lax.rem(x - piece % X + X, X)
    pick = jnp.logical_and(r_i % 8 == q_i // W, owner == (q_i % W) // wt).astype(f32)
    spread = dot(cg_all, pick, 0, 0, highest)
    l_i = lax.broadcasted_iota(jnp.int32, (128, cells), 0)
    w_i = lax.broadcasted_iota(jnp.int32, (128, cells), 1) % W
    spread = jnp.where(jnp.logical_and(l_i // L == w_i % wt, l_i < TILE), spread, 0.0)
    j_i = lax.broadcasted_iota(jnp.int32, (8, 128), 0)
    m_i = lax.broadcasted_iota(jnp.int32, (8, 128), 1)
    fold = jnp.logical_and(m_i % L == j_i, m_i < TILE).astype(f32)
    code = dot(fold, spread, 1, 0, highest)
    half_j = per_level(levels, lax.broadcasted_iota(jnp.int32, (8, cells), 0), L)
    code = code / half_j

    @pl.when(t == 0)
    def _():
        for k in range(2):
            first[k].wait()
            xb[k, 0] = xb[2, 0]
            xb[k, H] = xb[2, H]

    recv_if(dn_t, inner)
    recv_if(late_up, pass_dn)
    recv_if(late_dn, pass_up)
    pooled = pooled + frame_end(0, part[0] + taps(0, (0, 1)))
    pooled = (pooled + frame_end(1, part[1] + taps(1, (0,)))) * 0.25

    latent = dot(proj_t, pooled, 1, 1, highest)
    squashed = jnp.tanh(latent)
    step = (
        (code + 2.0 * commit_weight * offset_scale * squashed)
        * offset_scale
        * (1.0 - squashed * squashed)
        * scale
    )
    proj_part = dot(step, pooled, 1, 0, highest)
    pg_t = dot(proj_t, step, 0, 0, highest) * 0.25

    lane = lax.broadcasted_iota(jnp.int32, (C, W), 1)
    bias_sum = jnp.zeros((C, W), f32)
    for f in range(F):
        for h in range(R):
            g = pg_t[:, h * W : (h + 1) * W] * slope_t[f * R + h]
            bias_sum = bias_sum + g
            q0 = (f * R + h) * W
            gt[0:C, q0 : q0 + W] = jnp.where(lane == W - 1, 0.0, pltpu.roll(g, W - 1, 1)).astype(bf16)
            gt[C : 2 * C, q0 : q0 + W] = g.astype(bf16)
            gt[2 * C :, q0 : q0 + W] = jnp.where(lane == 0, 0.0, pltpu.roll(g, 1, 1)).astype(bf16)

    def small_space(d):
        return remote(sm_send, sm_recv.at[d], ss_s.at[d], ss_r.at[d], t, lax.rem(s + d, S))

    def small_x(d):
        return remote(sx_send, sx_recv.at[d], sx_s.at[d], sx_r.at[d], z * X + lax.rem(x + d, X), s)

    def small_z(d):
        return remote(sz_send, sz_recv.at[d], sz_s.at[d], sz_r.at[d], lax.rem(z + d, Z) * X + x, s)

    def core_copy(g):
        lanes = slice(g * G, (g + 1) * G)
        return remote(
            acc.at[1 - core, :, :, lanes], recv1.at[:, :, lanes],
            core_s.at[g], core_r.at[g], t, s + 1 - 2 * core,
        )

    def plane_copy(c, dy, dx):
        ty, tx, k = lax.rem(y + dy, Y), lax.rem(x + dx, X), dy * X + dx
        return remote(
            stage2.at[c, ty, tx], recv2.at[c, k], y_s.at[c, k], y_r.at[c, k],
            z * X + tx, ty * 2 + core,
        )

    def z_copy(to, slot):
        return remote(stage3.at[to], recv3.at[slot], tm_s.at[to], tm_r.at[slot], to * X + x, s)

    peers = [(dy, dx) for dy in range(Y) for dx in range(X) if dy or dx]
    chunks = sorted(range(Z), key=lambda c: -max(c, Z - 1 - c))

    def groups_of(c):
        return range(c * KZ // G, ((c + 1) * KZ - 1) // G + 1)

    order = []
    for c in chunks:
        order += [g for g in groups_of(c) if g not in order]
    sets = [order[k : k + 2] for k in range(0, len(order), 2)]

    def products(groups):
        rhs = jnp.concatenate(
            [xb[g // 3 : g // 3 + F, g % 3 : g % 3 + R].reshape(F * cells, C) for g in groups], 1
        )
        res = dot(gt[...], rhs, 1, 0)
        for n, g in enumerate(groups):
            for c in range(3):
                k0 = g * G + c * C
                for sp in range(S):
                    acc[sp % 2, sp // 2, :, k0 : k0 + C] = res[
                        c * C + sp * oc : c * C + (sp + 1) * oc, n * C : (n + 1) * C
                    ]
            core_copy(g).start()

    half_lane = lax.broadcasted_iota(jnp.int32, (oc // 2, 128), 1) < 64
    arrived = set()

    def fold_core(c):
        for g in groups_of(c):
            if g not in arrived:
                core_copy(g).wait_recv()
                arrived.add(g)
        for yy in range(Y):
            for xx in range(X):
                off = (c * X + xx) * KT
                base = off // 128 * 128
                wide = min(-(-KT // 128) * 128 + 128, KC - base)
                win = acc[core, yy, :, base : base + wide] + recv1[yy, :, base : base + wide]
                if off > base:
                    win = pltpu.roll(win, wide - (off - base), 1)
                pieces = [win[:, 128 * k : 128 * (k + 1)] for k in range(full)]
                if rest:
                    last = win[:, 128 * full : 128 * (full + 1)]
                    if folded:
                        last = jnp.where(
                            half_lane, last[: oc // 2], pltpu.roll(last[oc // 2 :], 64, 1)
                        )
                    pieces.append(last)
                block = jnp.concatenate(pieces, 0)
                sum2[c, yy, xx] = block
                stage2[c, yy, xx] = block.astype(link_type)
        for dy, dx in peers:
            plane_copy(c, dy, dx).start()

    def fold_plane(c):
        v = sum2[c, y, x]
        for dy, dx in peers:
            plane_copy(c, dy, dx).wait_recv()
            v = v + recv2[c, dy * X + dx].astype(f32)
        own3[c] = v
        stage3[c] = v.astype(link_type)
        start_if(z != c, z_copy(c, z))

    bias_part = dot(jnp.ones((8, W), f32), bias_sum, 1, 1, highest)
    sm_send[...] = jnp.where(lax.broadcasted_iota(jnp.int32, (8, C), 0) == L, bias_part, proj_part)
    for d in range(1, S):
        small_space(d).start()

    ready = {}
    computed = []
    waiting = list(chunks)
    for n, groups in enumerate(sets):
        products(groups)
        if ready.get("next") is not None:
            fold_core(ready.pop("next"))
        computed += groups
        if waiting and all(g in computed for g in groups_of(waiting[0])):
            ready["next"] = waiting.pop(0)
    if ready.get("next") is not None:
        fold_core(ready.pop("next"))
    for c in waiting:
        fold_core(c)

    sm = sm_send[...]
    for d in range(1, S):
        small_space(d).wait_recv()
        sm = sm + sm_recv[d]
    sx_send[...] = sm
    for d in range(1, X):
        small_x(d).start()
    for n, c in enumerate(chunks):
        fold_plane(c)
        if n == 0:
            for d in range(1, X):
                small_x(d).wait_recv()
                sm = sm + sx_recv[d]
            sz_send[...] = sm
            for d in range(1, Z):
                small_z(d).start()
    for d in range(1, Z):
        small_z(d).wait_recv()
        sm = sm + sz_recv[d]
    small_out[...] = sm

    res = own3[z]
    for d in range(1, Z):
        src = lax.rem(z + d, Z)
        z_copy(src, src).wait_recv()
        res = res + recv3[src].astype(f32)
    for k in range(full):
        weight_out[:, 128 * k : 128 * (k + 1)] = res[k * oc : (k + 1) * oc]
    if rest:
        last = res[full * oc :]
        if folded:
            last = jnp.concatenate([last, pltpu.roll(last, 64, 1)], 0)
        weight_out[:, 128 * full :] = last[:, :rest]

    sent_if(up_s, row_up)
    sent_if(dn_s, row_dn)
    for copy in (edge_lo, edge_hi, inner):
        sent_if(up_t, copy)
    sent_if(late_dn, pass_dn)
    sent_if(late_up, pass_up)
    for d in range(1, X):
        cgx_copy(d).wait_send()
        small_x(d).wait_send()
    for d in range(1, Z):
        cgz_copy(d).wait_send()
        small_z(d).wait_send()
    for d in range(1, S):
        small_space(d).wait_send()
    for g in range(KC // G):
        core_copy(g).wait_send()
    for c in range(Z):
        for dy, dx in peers:
            plane_copy(c, dy, dx).wait_send()
        sent_if(z != c, z_copy(c, z))


def finish_kernel(levels, centres, wg, small, quant_out, weight_out, proj_out, bias_out):
    L = levels.shape[0]
    lane = lax.broadcasted_iota(jnp.int32, centres.shape, 2)
    half = per_level(levels, lax.rem(lane, L), L)
    quant_out[...] = (centres[...].astype(f32) - half) / half
    weight_out[...] = wg[...]
    proj_out[...] = small[0:L]
    bias_out[...] = small[L : L + 1]


def on_device(T, S, frames, conv_weight, conv_bias, projection, levels, centres, code_grad):
    F, R, W, C = frames.shape
    KC = conv_weight.shape[0]
    KT = KC // T
    oc, Y, cells = C // S, S // 2, R * W
    Z, X = grid_of(T)
    PB = packed_rows(oc, KT)[3]
    L, TILE = levels.shape[0], code_grad.shape[2]
    scale = float(F * T * R * S * W) ** -0.5
    vmem = pl.BlockSpec(memory_space=pltpu.VMEM)
    dma = pltpu.SemaphoreType.DMA
    wg, small = pl.pallas_call(
        functools.partial(block_kernel, T, S, scale),
        out_shape=(
            jax.ShapeDtypeStruct((oc, KT), f32),
            jax.ShapeDtypeStruct((8, C), f32),
        ),
        in_specs=[pl.BlockSpec(memory_space=pl.ANY)] * 6,
        out_specs=(vmem, vmem),
        scratch_shapes=[
            pltpu.VMEM((F + 2, R + 2, W, C), bf16),
            pltpu.VMEM((KC, C), bf16),
            pltpu.VMEM((1, C), f32),
            pltpu.VMEM((L, C), f32),
            pltpu.SMEM((L,), jnp.int32),
            pltpu.VMEM((T, R, TILE), f32),
            pltpu.VMEM((Z, X, 8, 128), f32),
            pltpu.VMEM((X, Z, 8, 128), f32),
            pltpu.VMEM((Z, X, 8, 128), f32),
            pltpu.VMEM((8, C), f32),
            pltpu.VMEM((2, cells, 3 * C), f32),
            pltpu.VMEM((F * R, C, W), f32),
            pltpu.VMEM((3 * C, F * cells), bf16),
            pltpu.VMEM((2, Y, oc, KC), f32),
            pltpu.VMEM((Y, oc, KC), f32),
            pltpu.VMEM((Z, Y, X, PB, 128), f32),
            pltpu.VMEM((Z, Y, X, PB, 128), link_type),
            pltpu.VMEM((Z, Y * X, PB, 128), link_type),
            pltpu.VMEM((Z, PB, 128), f32),
            pltpu.VMEM((Z, PB, 128), link_type),
            pltpu.VMEM((Z, PB, 128), link_type),
            pltpu.VMEM((8, C), f32),
            pltpu.VMEM((S, 8, C), f32),
            pltpu.VMEM((8, C), f32),
            pltpu.VMEM((X, 8, C), f32),
            pltpu.VMEM((8, C), f32),
            pltpu.VMEM((Z, 8, C), f32),
            dma((8,)), pltpu.SemaphoreType.REGULAR((max(Z - 2, 1), 2)),
            dma((7,)), dma((7,)), dma((X,)), dma((X,)), dma((Z,)), dma((Z,)),
            dma((S,)), dma((S,)), dma((X,)), dma((X,)), dma((Z,)), dma((Z,)),
            dma((9,)), dma((9,)), dma((Z, Y * X)), dma((Z, Y * X)), dma((Z,)), dma((Z,)),
        ],
        compiler_params=pltpu.CompilerParams(
            collective_id=0, has_side_effects=True, vmem_limit_bytes=56 * 1024 * 1024
        ),
    )(frames, conv_weight, conv_bias.reshape(1, C), projection.T, levels, code_grad)
    quantized, wg, proj_grad, bias_grad = pl.pallas_call(
        finish_kernel,
        out_shape=(
            jax.ShapeDtypeStruct(centres.shape, f32),
            jax.ShapeDtypeStruct(wg.shape, f32),
            jax.ShapeDtypeStruct((L, C), f32),
            jax.ShapeDtypeStruct((1, C), f32),
        ),
        in_specs=[pl.BlockSpec(memory_space=pltpu.SMEM), vmem, vmem, vmem],
        out_specs=(vmem,) * 4,
    )(levels, centres, wg, small)
    return quantized, wg.T, proj_grad.T, bias_grad.reshape(C)


def solution(mesh):
    return jax.shard_map(
        functools.partial(on_device, mesh.shape["tm"], mesh.shape["space"]),
        mesh=mesh,
        in_specs=(
            P("tm", "space", None, None),
            P(),
            P(),
            P(),
            P(),
            P(None, "space", "tm"),
            P(None, "space", "tm"),
        ),
        out_specs=(P(None, "space", "tm"), P("tm", "space"), P(), P()),
        check_vma=False,
    )
```

time: 38.2 us -> 34.4 us (0.901)
  the two profiles are of different devices: /device:TPU:24 before, /device:TPU:0 now
where the time goes in v1:
time: 34.4 us; the launch traced here: 34.1 us
  Pallas kernels  33.5 us (97%)
  between operations  0.64 us (2%)
    pallas_call x1, Pallas kernels, on_device(): pl.pallas_call(functools.partial(block_kernel, T, S, scale), out_shape=(j...  32 us
    pallas_call x1, Pallas kernels, on_device(): pl.pallas_call(finish_kernel, out_shape=(jax.ShapeDtypeStruct(centres.sha...  1.5 us

profile of v1, /device:TPU:0, one launch (start us, length us, event | category | flops | bytes accessed | tf_op | source)
XLA Modules:
  0.0 34.1 jit_solution(2776088589381391701)
XLA Ops:
  0.6 32.0 %shard_map.102 = (f32[32,432]{1,0:T(8,128)}, f32[8,128]{1,0:T(8,128)}) custom-call(bf16[4,4,128,128]{3,2,1,0:T(8,128)(2,1)} %frames.1, bf16[3456,128]{1,0:T(8,128)(2,1)} %weight_in.1, f32[1,128]{1,0:T(1,128)} %bitcast.6, f32[6,128]{1,0:T(8,128)} %bitcast.5, s32[6]{0:T(128)} %levels.1, f32[8,4,96]{2,1,0:T(4,128)} %code_in.1), custom_call_target="tpu_custom_call" | custom-call | tf_op jit(solution)/shard_map/pallas_call | solution.py:498
  32.6 1.5 %shard_map.103 = (f32[8,4,96]{2,1,0:T(4,128)}, f32[32,432]{1,0:T(8,128)}, f32[6,128]{1,0:T(8,128)}, f32[1,128]{1,0:T(1,128)}) custom-call(s32[6]{0:T(128)} %levels.1, s32[8,4,96]{2,1,0:T(4,128)} %centres.1, f32[32,432]{1,0:T(8,128)} %get-tuple-element.10.wg, f32[8,128]{1,0:T(8,128)} %get-tuple-element.11.small), custom_call_target="tpu_custom_call" | custom-call | tf_op jit(solution)/shard_map/pallas_call | solution.py:543

commit v2 on v1

--- a/solution.py
+++ b/solution.py
@@ -45,8 +45,8 @@
     weight_out, small_out,
     xb, weight, bias, proj, levels, code_grad, cg_a, cg_b, cg_c, pscr, part, slope_t, gt, acc, recv1,
     sum2, stage2, recv2, own3, stage3, recv3,
-    sm_send, sm_recv, sx_send, sx_recv, sz_send, sz_recv,
-    local_sem, token, halo_s, halo_r, cx_s, cx_r, cz_s, cz_r, ss_s, ss_r, sx_s, sx_r, sz_s, sz_r,
+    sm_send, sm_recv, sz_send, sz_recv,
+    local_sem, token, halo_s, halo_r, cx_s, cx_r, cz_s, cz_r, ss_s, ss_r, sz_s, sz_r,
     core_s, core_r, y_s, y_r, tm_s, tm_r,
 ):
     Y = S // 2
@@ -82,15 +82,11 @@
 
     signal_if(turn_up, t + 1, s)
     signal_if(turn_dn, t - 1, s)
-    for dx in range(1, X):
-        signal(z * X + lax.rem(x + dx, X), s)
     signal_if(up_z, t + X, s)
     signal_if(dn_z, t - X, s)
-    for dy in range(1, Y):
-        for dx in range(1, X):
-            signal(z * X + lax.rem(x + dx, X), lax.rem(y + dy, Y) * 2 + core)
-    for d in range(1, S):
-        signal(t, lax.rem(s + d, S))
+    plane = [(dx, ds) for dx in range(X) for ds in range(S) if dx or ds]
+    for dx, ds in plane:
+        signal(z * X + lax.rem(x + dx, X), lax.rem(s + ds, S))
 
     own = pltpu.make_async_copy(frames, xb.at[2 : 2 + F, 1 : 1 + R], local_sem.at[0])
     first = [
@@ -133,7 +129,7 @@
     one = lambda c: jnp.where(c, 1, 0)
     pl.semaphore_wait(
         barrier,
-        (S - 1) + (X - 1) * Y + one(up_z) + one(dn_z) + one(turn_up) + one(turn_dn),
+        (S * X - 1) + one(up_z) + one(dn_z) + one(turn_up) + one(turn_dn),
     )
 
     def remote(src, dst, ss_, rs_, tt, sp):
@@ -179,35 +175,35 @@
     pass_up = halo(6, xb.at[0:2, R], xb.at[0:2, 0], t, s + 1)
     late_dn, late_up = jnp.logical_and(dn_t, dn_s), jnp.logical_and(dn_t, up_s)
 
+    rounds = max(Z - 2, 0)
+
+    def chain(side):
+        sends, gets, to = ((up_z, dn_z, t + X), (dn_z, up_z, t - X))[side]
+        for r in range(rounds):
+            @pl.when(gets)
+            def _():
+                pl.semaphore_wait(token.at[r, side], 1)
+
+            if r + 1 < rounds:
+                signal_if(sends, to, s, token.at[r + 1, side])
+
+    def cgz_start(upper):
+        for d in range(1, Z):
+            above = lax.rem(z + d, Z) > z
+            start_if(above if upper else jnp.logical_not(above), cgz_copy(d))
+
+    if rounds:
+        signal_if(up_z, t + X, s, token.at[0, 0])
+        signal_if(dn_z, t - X, s, token.at[0, 1])
     for d in range(1, X):
         cgx_copy(d).start()
     start_if(up_t, edge_lo)
     start_if(up_t, edge_hi)
     start_if(up_s, row_up)
     start_if(dn_s, row_dn)
-
-    def token_send(r):
-        signal_if(up_z, t + X, s, token.at[r, 0])
-        signal_if(dn_z, t - X, s, token.at[r, 1])
-
-    def token_wait(r):
-        @pl.when(dn_z)
-        def _():
-            pl.semaphore_wait(token.at[r, 0], 1)
-
-        @pl.when(up_z)
-        def _():
-            pl.semaphore_wait(token.at[r, 1], 1)
-
-    for r in range(max(Z - 2, 0)):
-        token_send(r)
-        token_wait(r)
-    for d in range(1, X):
-        cgx_copy(d).wait_recv()
-    for d in range(1, Z):
-        cgz_copy(d).start()
+    sent_if(up_t, edge_lo)
+    sent_if(up_t, edge_hi)
     start_if(up_t, inner)
-
     proj_load.wait()
     bias_load.wait()
     levels_load.wait()
@@ -244,6 +240,12 @@
     recv_if(up_s, row_dn)
     pooled = frame_end(2, taps(2, (0, 1, 2)))
 
+    chain(0)
+    for d in range(1, X):
+        cgx_copy(d).wait_recv()
+    cgz_start(False)
+    chain(1)
+    cgz_start(True)
     recv_if(dn_t, edge_lo)
     start_if(late_dn, pass_dn)
     recv_if(dn_t, edge_hi)
@@ -252,6 +254,20 @@
     part[0] = taps(0, (2,))
     part[1] = taps(1, (1, 2))
 
+    @pl.when(t == 0)
+    def _():
+        for k in range(2):
+            first[k].wait()
+            xb[k, 0] = xb[2, 0]
+            xb[k, H] = xb[2, H]
+
+    recv_if(dn_t, inner)
+    recv_if(late_up, pass_dn)
+    recv_if(late_dn, pass_up)
+    pooled = pooled + frame_end(0, part[0] + taps(0, (0, 1)))
+    pooled = (pooled + frame_end(1, part[1] + taps(1, (0,)))) * 0.25
+
+    latent = dot(proj_t, pooled, 1, 1, highest)
     cg_c[0] = cg_b[:, z]
     for d in range(1, Z):
         cgz_copy(d).wait_recv()
@@ -273,20 +289,6 @@
     half_j = per_level(levels, lax.broadcasted_iota(jnp.int32, (8, cells), 0), L)
     code = code / half_j
 
-    @pl.when(t == 0)
-    def _():
-        for k in range(2):
-            first[k].wait()
-            xb[k, 0] = xb[2, 0]
-            xb[k, H] = xb[2, H]
-
-    recv_if(dn_t, inner)
-    recv_if(late_up, pass_dn)
-    recv_if(late_dn, pass_up)
-    pooled = pooled + frame_end(0, part[0] + taps(0, (0, 1)))
-    pooled = (pooled + frame_end(1, part[1] + taps(1, (0,)))) * 0.25
-
-    latent = dot(proj_t, pooled, 1, 1, highest)
     squashed = jnp.tanh(latent)
     step = (
         (code + 2.0 * commit_weight * offset_scale * squashed)
@@ -308,26 +310,32 @@
             gt[C : 2 * C, q0 : q0 + W] = g.astype(bf16)
             gt[2 * C :, q0 : q0 + W] = jnp.where(lane == 0, 0.0, pltpu.roll(g, 1, 1)).astype(bf16)
 
-    def small_space(d):
-        return remote(sm_send, sm_recv.at[d], ss_s.at[d], ss_r.at[d], t, lax.rem(s + d, S))
-
-    def small_x(d):
-        return remote(sx_send, sx_recv.at[d], sx_s.at[d], sx_r.at[d], z * X + lax.rem(x + d, X), s)
+    def small_plane(k):
+        dx, ds = plane[k]
+        return remote(
+            sm_send, sm_recv.at[k], ss_s.at[k], ss_r.at[k],
+            z * X + lax.rem(x + dx, X), lax.rem(s + ds, S),
+        )
 
     def small_z(d):
         return remote(sz_send, sz_recv.at[d], sz_s.at[d], sz_r.at[d], lax.rem(z + d, Z) * X + x, s)
 
+
     def core_copy(g):
-        lanes = slice(g * G, (g + 1) * G)
+        lo, hi = units[g]
         return remote(
-            acc.at[1 - core, :, :, lanes], recv1.at[:, :, lanes],
-            core_s.at[g], core_r.at[g], t, s + 1 - 2 * core,
+            acc.at[1 - core, lo:hi], recv1.at[lo:hi], core_s.at[g], core_r.at[g],
+            t, s + 1 - 2 * core,
         )
+
+    units = [(k, k + 3) for k in range(0, KC // G, 3)]
+    spans = [(c, c + 1) for c in range(Z)]
 
     def plane_copy(c, dy, dx):
         ty, tx, k = lax.rem(y + dy, Y), lax.rem(x + dx, X), dy * X + dx
+        lo, hi = spans[c]
         return remote(
-            stage2.at[c, ty, tx], recv2.at[c, k], y_s.at[c, k], y_r.at[c, k],
+            stage2.at[ty, tx, lo:hi], recv2.at[k, lo:hi], y_s.at[c, k], y_r.at[c, k],
             z * X + tx, ty * 2 + core,
         )
 
@@ -345,34 +353,45 @@
         order += [g for g in groups_of(c) if g not in order]
     sets = [order[k : k + 2] for k in range(0, len(order), 2)]
 
+    done = set()
+
     def products(groups):
+        done.update(groups)
         rhs = jnp.concatenate(
             [xb[g // 3 : g // 3 + F, g % 3 : g % 3 + R].reshape(F * cells, C) for g in groups], 1
         )
         res = dot(gt[...], rhs, 1, 0)
         for n, g in enumerate(groups):
             for c in range(3):
-                k0 = g * G + c * C
                 for sp in range(S):
-                    acc[sp % 2, sp // 2, :, k0 : k0 + C] = res[
+                    acc[sp % 2, g, sp // 2, :, c * C : (c + 1) * C] = res[
                         c * C + sp * oc : c * C + (sp + 1) * oc, n * C : (n + 1) * C
                     ]
-            core_copy(g).start()
+        for u, (lo, hi) in enumerate(units):
+            if any(lo <= g < hi for g in groups) and done.issuperset(range(lo, hi)):
+                core_copy(u).start()
 
     half_lane = lax.broadcasted_iota(jnp.int32, (oc // 2, 128), 1) < 64
     arrived = set()
 
     def fold_core(c):
-        for g in groups_of(c):
-            if g not in arrived:
-                core_copy(g).wait_recv()
-                arrived.add(g)
+        for u, (lo, hi) in enumerate(units):
+            if u not in arrived and any(lo <= g < hi for g in groups_of(c)):
+                core_copy(u).wait_recv()
+                arrived.add(u)
         for yy in range(Y):
             for xx in range(X):
                 off = (c * X + xx) * KT
                 base = off // 128 * 128
                 wide = min(-(-KT // 128) * 128 + 128, KC - base)
-                win = acc[core, yy, :, base : base + wide] + recv1[yy, :, base : base + wide]
+                win = jnp.concatenate(
+                    [
+                        acc[core, k // 3, yy, :, k % 3 * C : (k % 3 + 1) * C]
+                        + recv1[k // 3, yy, :, k % 3 * C : (k % 3 + 1) * C]
+                        for k in range(base // C, (base + wide) // C)
+                    ],
+                    1,
+                )
                 if off > base:
                     win = pltpu.roll(win, wide - (off - base), 1)
                 pieces = [win[:, 128 * k : 128 * (k + 1)] for k in range(full)]
@@ -385,23 +404,28 @@
                     pieces.append(last)
                 block = jnp.concatenate(pieces, 0)
                 sum2[c, yy, xx] = block
-                stage2[c, yy, xx] = block.astype(link_type)
-        for dy, dx in peers:
-            plane_copy(c, dy, dx).start()
+                stage2[yy, xx, c] = block.astype(link_type)
+        for k, (lo, hi) in enumerate(spans):
+            if c == hi - 1:
+                for dy, dx in peers:
+                    plane_copy(k, dy, dx).start()
 
     def fold_plane(c):
         v = sum2[c, y, x]
+        for k, (lo, hi) in enumerate(spans):
+            if c == lo:
+                for dy, dx in peers:
+                    plane_copy(k, dy, dx).wait_recv()
         for dy, dx in peers:
-            plane_copy(c, dy, dx).wait_recv()
-            v = v + recv2[c, dy * X + dx].astype(f32)
+            v = v + recv2[dy * X + dx, c].astype(f32)
         own3[c] = v
         stage3[c] = v.astype(link_type)
         start_if(z != c, z_copy(c, z))
 
     bias_part = dot(jnp.ones((8, W), f32), bias_sum, 1, 1, highest)
     sm_send[...] = jnp.where(lax.broadcasted_iota(jnp.int32, (8, C), 0) == L, bias_part, proj_part)
-    for d in range(1, S):
-        small_space(d).start()
+    for k in range(len(plane)):
+        small_plane(k).start()
 
     ready = {}
     computed = []
@@ -419,21 +443,14 @@
         fold_core(c)
 
     sm = sm_send[...]
-    for d in range(1, S):
-        small_space(d).wait_recv()
-        sm = sm + sm_recv[d]
-    sx_send[...] = sm
-    for d in range(1, X):
-        small_x(d).start()
-    for n, c in enumerate(chunks):
+    for k in range(len(plane)):
+        small_plane(k).wait_recv()
+        sm = sm + sm_recv[k]
+    sz_send[...] = sm
+    for d in range(1, Z):
+        small_z(d).start()
+    for c in chunks:
         fold_plane(c)
-        if n == 0:
-            for d in range(1, X):
-                small_x(d).wait_recv()
-                sm = sm + sx_recv[d]
-            sz_send[...] = sm
-            for d in range(1, Z):
-                small_z(d).start()
     for d in range(1, Z):
         small_z(d).wait_recv()
         sm = sm + sz_recv[d]
@@ -454,23 +471,22 @@
 
     sent_if(up_s, row_up)
     sent_if(dn_s, row_dn)
-    for copy in (edge_lo, edge_hi, inner):
-        sent_if(up_t, copy)
+    sent_if(up_t, inner)
     sent_if(late_dn, pass_dn)
     sent_if(late_up, pass_up)
     for d in range(1, X):
         cgx_copy(d).wait_send()
-        small_x(d).wait_send()
     for d in range(1, Z):
         cgz_copy(d).wait_send()
         small_z(d).wait_send()
-    for d in range(1, S):
-        small_space(d).wait_send()
-    for g in range(KC // G):
-        core_copy(g).wait_send()
+    for k in range(len(plane)):
+        small_plane(k).wait_send()
+    for u in range(len(units)):
+        core_copy(u).wait_send()
+    for k in range(len(spans)):
+        for dy, dx in peers:
+            plane_copy(k, dy, dx).wait_send()
     for c in range(Z):
-        for dy, dx in peers:
-            plane_copy(c, dy, dx).wait_send()
         sent_if(z != c, z_copy(c, z))
 
 
@@ -498,8 +514,8 @@
     wg, small = pl.pallas_call(
         functools.partial(block_kernel, T, S, scale),
         out_shape=(
-            jax.ShapeDtypeStruct((oc, KT), f32),
-            jax.ShapeDtypeStruct((8, C), f32),
+            pltpu.VMEM((oc, KT), f32),
+            pltpu.VMEM((8, C), f32),
         ),
         in_specs=[pl.BlockSpec(memory_space=pl.ANY)] * 6,
         out_specs=(vmem, vmem),
@@ -517,23 +533,21 @@
             pltpu.VMEM((2, cells, 3 * C), f32),
             pltpu.VMEM((F * R, C, W), f32),
             pltpu.VMEM((3 * C, F * cells), bf16),
-            pltpu.VMEM((2, Y, oc, KC), f32),
-            pltpu.VMEM((Y, oc, KC), f32),
+            pltpu.VMEM((2, 9, Y, oc, 3 * C), f32),
+            pltpu.VMEM((9, Y, oc, 3 * C), f32),
             pltpu.VMEM((Z, Y, X, PB, 128), f32),
-            pltpu.VMEM((Z, Y, X, PB, 128), link_type),
-            pltpu.VMEM((Z, Y * X, PB, 128), link_type),
+            pltpu.VMEM((Y, X, Z, PB, 128), link_type),
+            pltpu.VMEM((Y * X, Z, PB, 128), link_type),
             pltpu.VMEM((Z, PB, 128), f32),
             pltpu.VMEM((Z, PB, 128), link_type),
             pltpu.VMEM((Z, PB, 128), link_type),
             pltpu.VMEM((8, C), f32),
-            pltpu.VMEM((S, 8, C), f32),
-            pltpu.VMEM((8, C), f32),
-            pltpu.VMEM((X, 8, C), f32),
+            pltpu.VMEM((S * X, 8, C), f32),
             pltpu.VMEM((8, C), f32),
             pltpu.VMEM((Z, 8, C), f32),
             dma((8,)), pltpu.SemaphoreType.REGULAR((max(Z - 2, 1), 2)),
             dma((7,)), dma((7,)), dma((X,)), dma((X,)), dma((Z,)), dma((Z,)),
-            dma((S,)), dma((S,)), dma((X,)), dma((X,)), dma((Z,)), dma((Z,)),
+            dma((S * X,)), dma((S * X,)), dma((Z,)), dma((Z,)),
             dma((9,)), dma((9,)), dma((Z, Y * X)), dma((Z, Y * X)), dma((Z,)), dma((Z,)),
         ],
         compiler_params=pltpu.CompilerParams(
@@ -550,7 +564,11 @@
         ),
         in_specs=[pl.BlockSpec(memory_space=pltpu.SMEM), vmem, vmem, vmem],
         out_specs=(vmem,) * 4,
-    )(levels, centres, wg, small)
+    )(
+        levels, centres,
+        pltpu.with_memory_space_constraint(wg, pltpu.VMEM),
+        pltpu.with_memory_space_constraint(small, pltpu.VMEM),
+    )
     return quantized, wg.T, proj_grad.T, bias_grad.reshape(C)
 
 

time: 34.4 us -> 32.1 us (0.933)
  Pallas kernels: 33.5 us -> 31.2 us
    pallas_call x1, Pallas kernels: 32 us -> 29.8 us  [on_device(): pl.pallas_call(functools.partial(block_kernel, T, S, scale), out_shape=(p...]
where the time goes in v2:
time: 32.1 us; the launch traced here: 31.9 us
  Pallas kernels  31.2 us (97%)
  between operations  0.64 us (2%)
    pallas_call x1, Pallas kernels, on_device(): pl.pallas_call(functools.partial(block_kernel, T, S, scale), out_shape=(p...  29.8 us
    pallas_call x1, Pallas kernels, on_device(): pl.pallas_call(finish_kernel, out_shape=(jax.ShapeDtypeStruct(centres.sha...  1.38 us

profile of v2, /device:TPU:0, one launch (start us, length us, event | category | flops | bytes accessed | tf_op | source)
XLA Modules:
  0.0 31.9 jit_solution(12338375324274748537)
XLA Ops:
  0.6 29.8 %shard_map.102 = (f32[32,432]{1,0:T(8,128)S(1)}, f32[8,128]{1,0:T(8,128)S(1)}) custom-call(bf16[4,4,128,128]{3,2,1,0:T(8,128)(2,1)} %frames.1, bf16[3456,128]{1,0:T(8,128)(2,1)} %weight_in.1, f32[1,128]{1,0:T(1,128)} %bitcast.6, f32[6,128]{1,0:T(8,128)} %bitcast.5, s32[6]{0:T(128)} %levels.1, f32[8,4,96]{2,1,0:T(4,128)} %code_in.1), custom_call_target="tpu_custom_call" | custom-call | tf_op jit(solution)/shard_map/pallas_call | solution.py:514
  30.5 1.4 %shard_map.103 = (f32[8,4,96]{2,1,0:T(4,128)}, f32[32,432]{1,0:T(8,128)}, f32[6,128]{1,0:T(8,128)}, f32[1,128]{1,0:T(1,128)}) custom-call(s32[6]{0:T(128)} %levels.1, s32[8,4,96]{2,1,0:T(4,128)} %centres.1, f32[32,432]{1,0:T(8,128)S(1)} %get-tuple-element.10.wg, f32[8,128]{1,0:T(8,128)S(1)} %get-tuple-element.11.small), custom_call_target="tpu_custom_call" | custom-call | tf_op jit(solution)/shard_map/pallas_call | solution.py:557

commit v3 on v2

--- a/solution.py
+++ b/solution.py
@@ -41,9 +41,9 @@
 
 def block_kernel(
     T, S, scale,
-    frames, weight_in, bias_in, proj_in, levels_in, code_in,
-    weight_out, small_out,
-    xb, weight, bias, proj, levels, code_grad, cg_a, cg_b, cg_c, pscr, part, slope_t, gt, acc, recv1,
+    frames, weight_in, bias_in, proj_in, levels_in, code_in, centres_in,
+    weight_out, small_out, quant_out,
+    centres, xb, weight, bias, proj, levels, code_grad, cg_a, cg_b, cg_c, pscr, part, slope_t, gt, acc, recv1,
     sum2, stage2, recv2, own3, stage3, recv3,
     sm_send, sm_recv, sz_send, sz_recv,
     local_sem, token, halo_s, halo_r, cx_s, cx_r, cz_s, cz_r, ss_s, ss_r, sz_s, sz_r,
@@ -98,12 +98,14 @@
     bias_load = pltpu.make_async_copy(bias_in, bias, local_sem.at[5])
     levels_load = pltpu.make_async_copy(levels_in, levels, local_sem.at[6])
     weight_load = pltpu.make_async_copy(weight_in, weight, local_sem.at[7])
+    centres_load = pltpu.make_async_copy(centres_in, centres, local_sem.at[8])
     code_load.start()
     own.start()
     weight_load.start()
     proj_load.start()
     bias_load.start()
     levels_load.start()
+    centres_load.start()
 
     @pl.when(t == 0)
     def _():
@@ -207,6 +209,10 @@
     proj_load.wait()
     bias_load.wait()
     levels_load.wait()
+    centres_load.wait()
+    column = lax.broadcasted_iota(jnp.int32, centres.shape, 2)
+    half = per_level(levels, lax.rem(column, L), L)
+    quant_out[...] = (centres[...].astype(f32) - half) / half
     pscr[0:L] = proj[...]
     proj_t = pscr[...]
     row = lax.broadcasted_iota(jnp.int32, (cells, C), 0) % W
@@ -328,7 +334,18 @@
             t, s + 1 - 2 * core,
         )
 
-    units = [(k, k + 3) for k in range(0, KC // G, 3)]
+    def groups_of(c):
+        return range(c * KZ // G, ((c + 1) * KZ - 1) // G + 1)
+
+    chunks = sorted(range(Z), key=lambda c: -max(c, Z - 1 - c))
+    order, units = [], []
+    for c in chunks:
+        fresh = [g for g in groups_of(c) if g not in order]
+        order += fresh
+        if fresh:
+            units.append((fresh[0], fresh[-1] + 1))
+    sets = [order[k : k + 2] for k in range(0, len(order), 2)]
+
     spans = [(c, c + 1) for c in range(Z)]
 
     def plane_copy(c, dy, dx):
@@ -343,20 +360,7 @@
         return remote(stage3.at[to], recv3.at[slot], tm_s.at[to], tm_r.at[slot], to * X + x, s)
 
     peers = [(dy, dx) for dy in range(Y) for dx in range(X) if dy or dx]
-    chunks = sorted(range(Z), key=lambda c: -max(c, Z - 1 - c))
-
-    def groups_of(c):
-        return range(c * KZ // G, ((c + 1) * KZ - 1) // G + 1)
-
-    order = []
-    for c in chunks:
-        order += [g for g in groups_of(c) if g not in order]
-    sets = [order[k : k + 2] for k in range(0, len(order), 2)]
-
-    done = set()
-
     def products(groups):
-        done.update(groups)
         rhs = jnp.concatenate(
             [xb[g // 3 : g // 3 + F, g % 3 : g % 3 + R].reshape(F * cells, C) for g in groups], 1
         )
@@ -368,7 +372,7 @@
                         c * C + sp * oc : c * C + (sp + 1) * oc, n * C : (n + 1) * C
                     ]
         for u, (lo, hi) in enumerate(units):
-            if any(lo <= g < hi for g in groups) and done.issuperset(range(lo, hi)):
+            if max(order.index(g) for g in range(lo, hi)) in [order.index(g) for g in groups]:
                 core_copy(u).start()
 
     half_lane = lax.broadcasted_iota(jnp.int32, (oc // 2, 128), 1) < 64
@@ -427,18 +431,12 @@
     for k in range(len(plane)):
         small_plane(k).start()
 
-    ready = {}
-    computed = []
     waiting = list(chunks)
     for n, groups in enumerate(sets):
         products(groups)
-        if ready.get("next") is not None:
-            fold_core(ready.pop("next"))
-        computed += groups
-        if waiting and all(g in computed for g in groups_of(waiting[0])):
-            ready["next"] = waiting.pop(0)
-    if ready.get("next") is not None:
-        fold_core(ready.pop("next"))
+        known = sum((sets[k] for k in range(n + 1 - 1)), [])
+        while waiting and all(g in known for g in groups_of(waiting[0])):
+            fold_core(waiting.pop(0))
     for c in waiting:
         fold_core(c)
 
@@ -490,11 +488,9 @@
         sent_if(z != c, z_copy(c, z))
 
 
-def finish_kernel(levels, centres, wg, small, quant_out, weight_out, proj_out, bias_out):
-    L = levels.shape[0]
-    lane = lax.broadcasted_iota(jnp.int32, centres.shape, 2)
-    half = per_level(levels, lax.rem(lane, L), L)
-    quant_out[...] = (centres[...].astype(f32) - half) / half
+def finish_kernel(quant, wg, small, quant_out, weight_out, proj_out, bias_out):
+    L = proj_out.shape[0]
+    quant_out[...] = quant[...]
     weight_out[...] = wg[...]
     proj_out[...] = small[0:L]
     bias_out[...] = small[L : L + 1]
@@ -511,15 +507,17 @@
     scale = float(F * T * R * S * W) ** -0.5
     vmem = pl.BlockSpec(memory_space=pltpu.VMEM)
     dma = pltpu.SemaphoreType.DMA
-    wg, small = pl.pallas_call(
+    held = pl.pallas_call(
         functools.partial(block_kernel, T, S, scale),
         out_shape=(
             pltpu.VMEM((oc, KT), f32),
             pltpu.VMEM((8, C), f32),
+            pltpu.VMEM(centres.shape, f32),
         ),
-        in_specs=[pl.BlockSpec(memory_space=pl.ANY)] * 6,
-        out_specs=(vmem, vmem),
+        in_specs=[pl.BlockSpec(memory_space=pl.ANY)] * 7,
+        out_specs=(vmem,) * 3,
         scratch_shapes=[
+            pltpu.VMEM(centres.shape, jnp.int32),
             pltpu.VMEM((F + 2, R + 2, W, C), bf16),
             pltpu.VMEM((KC, C), bf16),
             pltpu.VMEM((1, C), f32),
@@ -545,7 +543,7 @@
             pltpu.VMEM((S * X, 8, C), f32),
             pltpu.VMEM((8, C), f32),
             pltpu.VMEM((Z, 8, C), f32),
-            dma((8,)), pltpu.SemaphoreType.REGULAR((max(Z - 2, 1), 2)),
+            dma((9,)), pltpu.SemaphoreType.REGULAR((max(Z - 2, 1), 2)),
             dma((7,)), dma((7,)), dma((X,)), dma((X,)), dma((Z,)), dma((Z,)),
             dma((S * X,)), dma((S * X,)), dma((Z,)), dma((Z,)),
             dma((9,)), dma((9,)), dma((Z, Y * X)), dma((Z, Y * X)), dma((Z,)), dma((Z,)),
@@ -553,7 +551,10 @@
         compiler_params=pltpu.CompilerParams(
             collective_id=0, has_side_effects=True, vmem_limit_bytes=56 * 1024 * 1024
         ),
-    )(frames, conv_weight, conv_bias.reshape(1, C), projection.T, levels, code_grad)
+    )(frames, conv_weight, conv_bias.reshape(1, C), projection.T, levels, code_grad, centres)
+    wg, small, quantized = (
+        pltpu.with_memory_space_constraint(v, pltpu.VMEM) for v in held
+    )
     quantized, wg, proj_grad, bias_grad = pl.pallas_call(
         finish_kernel,
         out_shape=(
@@ -562,13 +563,9 @@
             jax.ShapeDtypeStruct((L, C), f32),
             jax.ShapeDtypeStruct((1, C), f32),
         ),
-        in_specs=[pl.BlockSpec(memory_space=pltpu.SMEM), vmem, vmem, vmem],
+        in_specs=[vmem] * 3,
         out_specs=(vmem,) * 4,
-    )(
-        levels, centres,
-        pltpu.with_memory_space_constraint(wg, pltpu.VMEM),
-        pltpu.with_memory_space_constraint(small, pltpu.VMEM),
-    )
+    )(quantized, wg, small)
     return quantized, wg.T, proj_grad.T, bias_grad.reshape(C)
 
 

time: 32.1 us -> 30.7 us (0.956)
  Pallas kernels: 31.2 us -> 29.9 us
    pallas_call x1, Pallas kernels: 1.38 us -> 0.64 us  [on_device(): pl.pallas_call(finish_kernel, out_shape=(jax.ShapeDtypeStruct(centres.sha...]
    pallas_call x1, Pallas kernels: 29.8 us -> 29.2 us  [on_device(): pl.pallas_call(functools.partial(block_kernel, T, S, scale), out_shape=(p...]
where the time goes in v3:
time: 30.7 us; the launch traced here: 30.5 us
  Pallas kernels  29.9 us (97%)
  between operations  0.64 us (2%)
    pallas_call x1, Pallas kernels, on_device(): pl.pallas_call(functools.partial(block_kernel, T, S, scale), out_shape=(p...  29.2 us
    pallas_call x1, Pallas kernels, on_device(): pl.pallas_call(finish_kernel, out_shape=(jax.ShapeDtypeStruct(centres.sha...  0.64 us

profile of v3, /device:TPU:0, one launch (start us, length us, event | category | flops | bytes accessed | tf_op | source)
XLA Modules:
  0.0 30.5 jit_solution(3352228307635803385)
XLA Ops:
  0.6 29.2 %shard_map.102 = (f32[32,432]{1,0:T(8,128)S(1)}, f32[8,128]{1,0:T(8,128)S(1)}, f32[8,4,96]{2,1,0:T(4,128)S(1)}) custom-call(bf16[4,4,128,128]{3,2,1,0:T(8,128)(2,1)} %frames.1, bf16[3456,128]{1,0:T(8,128)(2,1)} %weight_in.1, f32[1,128]{1,0:T(1,128)} %bitcast.6, f32[6,128]{1,0:T(8,128)} %bitcast.5, s32[6]{0:T(128)} %levels_in.1, f32[8,4,96]{2,1,0:T(4,128)} %code_in.1, ...), custom_call_target="tpu_custom_call" | custom-call | tf_op jit(solution)/shard_map/pallas_call | solution.py:510
  29.9 0.6 %shard_map.103 = (f32[8,4,96]{2,1,0:T(4,128)}, f32[32,432]{1,0:T(8,128)}, f32[6,128]{1,0:T(8,128)}, f32[1,128]{1,0:T(1,128)}) custom-call(f32[8,4,96]{2,1,0:T(4,128)S(1)} %get-tuple-element.11.quant, f32[32,432]{1,0:T(8,128)S(1)} %get-tuple-element.12.wg, f32[8,128]{1,0:T(8,128)S(1)} %get-tuple-element.13.small), custom_call_target="tpu_custom_call" | custom-call | tf_op jit(solution)/shard_map/pallas_call | solution.py:558

commit v4 on v3

--- a/solution.py
+++ b/solution.py
@@ -203,9 +203,6 @@
     start_if(up_t, edge_hi)
     start_if(up_s, row_up)
     start_if(dn_s, row_dn)
-    sent_if(up_t, edge_lo)
-    sent_if(up_t, edge_hi)
-    start_if(up_t, inner)
     proj_load.wait()
     bias_load.wait()
     levels_load.wait()
@@ -215,50 +212,74 @@
     quant_out[...] = (centres[...].astype(f32) - half) / half
     pscr[0:L] = proj[...]
     proj_t = pscr[...]
-    row = lax.broadcasted_iota(jnp.int32, (cells, C), 0) % W
-
-    def taps(f, times):
+    def taps(jobs, times):
         slabs = []
         weights = []
         for a in times:
             for b in range(3):
-                slabs.append(xb[f + a, b : b + R].reshape(cells, C))
+                slabs.append(
+                    jnp.concatenate(
+                        [xb[f + a, lo + b : hi + b].reshape((hi - lo) * W, C) for f, lo, hi in jobs], 0
+                    )
+                )
                 k0 = (a * 3 + b) * G
                 weights.append(
                     jnp.concatenate([weight[k0 + c * C : k0 + (c + 1) * C] for c in range(3)], 1)
                 )
         return dot(jnp.concatenate(slabs, 1), jnp.concatenate(weights, 0), 1, 0)
 
-    def frame_end(f, out):
+    sums = {}
+
+    def rows_end(out, jobs):
+        size = out.shape[0]
+        row = lax.broadcasted_iota(jnp.int32, (size, C), 0) % W
         left = jnp.where(row == 0, 0.0, pltpu.roll(out[:, 0:C], 1, 0))
-        right = jnp.where(row == W - 1, 0.0, pltpu.roll(out[:, 2 * C :], cells - 1, 0))
+        right = jnp.where(row == W - 1, 0.0, pltpu.roll(out[:, 2 * C :], size - 1, 0))
         pre = out[:, C : 2 * C] + bias[...] + left + right
         sig = 1.0 / (1.0 + jnp.exp(-pre))
         act = (pre * sig).astype(bf16).astype(f32)
         slope = sig * (1.0 + pre * (1.0 - sig))
-        for h in range(R):
-            slope_t[f * R + h] = slope[h * W : (h + 1) * W].T
-        return act
+        lines = [(f, h) for f, lo, hi in jobs for h in range(lo, hi)]
+        for n, (f, h) in enumerate(lines):
+            slope_t[f * R + h] = slope[n * W : (n + 1) * W].T
+            line = act[n * W : (n + 1) * W]
+            sums[h] = sums[h] + line if h in sums else line
+
+    inside = lambda f: [(f, 1, R - 1)]
+    outside = lambda f: [(f, 0, 1), (f, R - 1, R)]
+
+    def own_taps(place):
+        for k, times in ((0, (2,)), (1, (1, 2))):
+            out = taps(place(k), times)
+            at = 0
+            for _, lo, hi in place(k):
+                part[k, lo * W : hi * W] = out[at : at + (hi - lo) * W]
+                at += (hi - lo) * W
+
+    def frames_of(place):
+        return sum((place(f) for f in range(2, F)), [])
 
     own.wait()
     weight_load.wait()
+    rows_end(taps(frames_of(inside), (0, 1, 2)), frames_of(inside))
+    own_taps(inside)
+    sent_if(up_t, edge_lo)
+    sent_if(up_t, edge_hi)
+    start_if(up_t, inner)
     recv_if(dn_s, row_up)
     recv_if(up_s, row_dn)
-    pooled = frame_end(2, taps(2, (0, 1, 2)))
-
+    rows_end(taps(frames_of(outside), (0, 1, 2)), frames_of(outside))
+    recv_if(dn_t, edge_lo)
+    start_if(late_dn, pass_dn)
+    recv_if(dn_t, edge_hi)
+    start_if(late_up, pass_up)
     chain(0)
     for d in range(1, X):
         cgx_copy(d).wait_recv()
     cgz_start(False)
     chain(1)
     cgz_start(True)
-    recv_if(dn_t, edge_lo)
-    start_if(late_dn, pass_dn)
-    recv_if(dn_t, edge_hi)
-    start_if(late_up, pass_up)
-    pooled = pooled + frame_end(3, taps(3, (0, 1, 2)))
-    part[0] = taps(0, (2,))
-    part[1] = taps(1, (1, 2))
+    own_taps(outside)
 
     @pl.when(t == 0)
     def _():
@@ -270,8 +291,9 @@
     recv_if(dn_t, inner)
     recv_if(late_up, pass_dn)
     recv_if(late_dn, pass_up)
-    pooled = pooled + frame_end(0, part[0] + taps(0, (0, 1)))
-    pooled = (pooled + frame_end(1, part[1] + taps(1, (0,)))) * 0.25
+    rows_end(part[0] + taps([(0, 0, R)], (0, 1)), [(0, 0, R)])
+    rows_end(part[1] + taps([(1, 0, R)], (0,)), [(1, 0, R)])
+    pooled = jnp.concatenate([sums[h] for h in range(R)], 0) * 0.25
 
     latent = dot(proj_t, pooled, 1, 1, highest)
     cg_c[0] = cg_b[:, z]
@@ -302,7 +324,6 @@
         * (1.0 - squashed * squashed)
         * scale
     )
-    proj_part = dot(step, pooled, 1, 0, highest)
     pg_t = dot(proj_t, step, 0, 0, highest) * 0.25
 
     lane = lax.broadcasted_iota(jnp.int32, (C, W), 1)
@@ -426,14 +447,15 @@
         stage3[c] = v.astype(link_type)
         start_if(z != c, z_copy(c, z))
 
-    bias_part = dot(jnp.ones((8, W), f32), bias_sum, 1, 1, highest)
-    sm_send[...] = jnp.where(lax.broadcasted_iota(jnp.int32, (8, C), 0) == L, bias_part, proj_part)
-    for k in range(len(plane)):
-        small_plane(k).start()
-
     waiting = list(chunks)
     for n, groups in enumerate(sets):
         products(groups)
+        if n == 1:
+            proj_part = dot(step, pooled, 1, 0, highest)
+            bias_part = dot(jnp.ones((8, W), f32), bias_sum, 1, 1, highest)
+            sm_send[...] = jnp.where(lax.broadcasted_iota(jnp.int32, (8, C), 0) == L, bias_part, proj_part)
+            for k in range(len(plane)):
+                small_plane(k).start()
         known = sum((sets[k] for k in range(n + 1 - 1)), [])
         while waiting and all(g in known for g in groups_of(waiting[0])):
             fold_core(waiting.pop(0))

time: 30.7 us -> 30 us (0.977)
  Pallas kernels: 29.9 us -> 29.1 us
    pallas_call x1, Pallas kernels: 29.2 us -> 28.5 us  [on_device(): pl.pallas_call(functools.partial(block_kernel, T, S, scale), out_shape=(p...]
where the time goes in v4:
time: 30 us; the launch traced here: 29.8 us
  Pallas kernels  29.1 us (97%)
  between operations  0.64 us (2%)
    pallas_call x1, Pallas kernels, on_device(): pl.pallas_call(functools.partial(block_kernel, T, S, scale), out_shape=(p...  28.5 us
    pallas_call x1, Pallas kernels, on_device(): pl.pallas_call(finish_kernel, out_shape=(jax.ShapeDtypeStruct(centres.sha...  0.64 us

profile of v4, /device:TPU:0, one launch (start us, length us, event | category | flops | bytes accessed | tf_op | source)
XLA Modules:
  0.0 29.8 jit_solution(16665715411272838226)
XLA Ops:
  0.6 28.5 %shard_map.102 = (f32[32,432]{1,0:T(8,128)S(1)}, f32[8,128]{1,0:T(8,128)S(1)}, f32[8,4,96]{2,1,0:T(4,128)S(1)}) custom-call(bf16[4,4,128,128]{3,2,1,0:T(8,128)(2,1)} %frames.1, bf16[3456,128]{1,0:T(8,128)(2,1)} %weight_in.1, f32[1,128]{1,0:T(1,128)} %bitcast.6, f32[6,128]{1,0:T(8,128)} %bitcast.5, s32[6]{0:T(128)} %levels_in.1, f32[8,4,96]{2,1,0:T(4,128)} %code_in.1, ...), custom_call_target="tpu_custom_call" | custom-call | tf_op jit(solution)/shard_map/pallas_call | solution.py:532
  29.1 0.6 %shard_map.103 = (f32[8,4,96]{2,1,0:T(4,128)}, f32[32,432]{1,0:T(8,128)}, f32[6,128]{1,0:T(8,128)}, f32[1,128]{1,0:T(1,128)}) custom-call(f32[8,4,96]{2,1,0:T(4,128)S(1)} %get-tuple-element.11.quant, f32[32,432]{1,0:T(8,128)S(1)} %get-tuple-element.12.wg, f32[8,128]{1,0:T(8,128)S(1)} %get-tuple-element.13.small), custom_call_target="tpu_custom_call" | custom-call | tf_op jit(solution)/shard_map/pallas_call | solution.py:580

commit v5 on v4

--- a/solution.py
+++ b/solution.py
@@ -281,6 +281,20 @@
     cgz_start(True)
     own_taps(outside)
 
+    wt = TILE // L
+    r_i = lax.broadcasted_iota(jnp.int32, (T * 8, cells), 0)
+    q_i = lax.broadcasted_iota(jnp.int32, (T * 8, cells), 1)
+    piece = r_i // 8
+    owner = lax.rem(z - piece // X + Z, Z) * X + lax.rem(x - piece % X + X, X)
+    pick = jnp.logical_and(r_i % 8 == q_i // W, owner == (q_i % W) // wt).astype(f32)
+    l_i = lax.broadcasted_iota(jnp.int32, (128, cells), 0)
+    w_i = lax.broadcasted_iota(jnp.int32, (128, cells), 1) % W
+    keep = jnp.logical_and(l_i // L == w_i % wt, l_i < TILE)
+    j_i = lax.broadcasted_iota(jnp.int32, (8, 128), 0)
+    m_i = lax.broadcasted_iota(jnp.int32, (8, 128), 1)
+    fold = jnp.logical_and(m_i % L == j_i, m_i < TILE).astype(f32)
+    half_j = per_level(levels, lax.broadcasted_iota(jnp.int32, (8, cells), 0), L)
+
     @pl.when(t == 0)
     def _():
         for k in range(2):
@@ -296,28 +310,16 @@
     pooled = jnp.concatenate([sums[h] for h in range(R)], 0) * 0.25
 
     latent = dot(proj_t, pooled, 1, 1, highest)
+    squashed = jnp.tanh(latent)
     cg_c[0] = cg_b[:, z]
     for d in range(1, Z):
         cgz_copy(d).wait_recv()
-    wt = TILE // L
     cg_all = cg_c[...].reshape(T * 8, 128)
-    r_i = lax.broadcasted_iota(jnp.int32, (T * 8, cells), 0)
-    q_i = lax.broadcasted_iota(jnp.int32, (T * 8, cells), 1)
-    piece = r_i // 8
-    owner = lax.rem(z - piece // X + Z, Z) * X + lax.rem(x - piece % X + X, X)
-    pick = jnp.logical_and(r_i % 8 == q_i // W, owner == (q_i % W) // wt).astype(f32)
     spread = dot(cg_all, pick, 0, 0, highest)
-    l_i = lax.broadcasted_iota(jnp.int32, (128, cells), 0)
-    w_i = lax.broadcasted_iota(jnp.int32, (128, cells), 1) % W
-    spread = jnp.where(jnp.logical_and(l_i // L == w_i % wt, l_i < TILE), spread, 0.0)
-    j_i = lax.broadcasted_iota(jnp.int32, (8, 128), 0)
-    m_i = lax.broadcasted_iota(jnp.int32, (8, 128), 1)
-    fold = jnp.logical_and(m_i % L == j_i, m_i < TILE).astype(f32)
+    spread = jnp.where(keep, spread, 0.0)
     code = dot(fold, spread, 1, 0, highest)
-    half_j = per_level(levels, lax.broadcasted_iota(jnp.int32, (8, cells), 0), L)
     code = code / half_j
 
-    squashed = jnp.tanh(latent)
     step = (
         (code + 2.0 * commit_weight * offset_scale * squashed)
         * offset_scale

time: 30 us -> 30 us (level)
  no operation moved by 1% of the time
where the time goes in v5:
time: 30 us; the launch traced here: 29.8 us
  Pallas kernels  29.1 us (97%)
  between operations  0.64 us (2%)
    pallas_call x1, Pallas kernels, on_device(): pl.pallas_call(functools.partial(block_kernel, T, S, scale), out_shape=(p...  28.5 us
    pallas_call x1, Pallas kernels, on_device(): pl.pallas_call(finish_kernel, out_shape=(jax.ShapeDtypeStruct(centres.sha...  0.64 us

profile of v5, /device:TPU:0, one launch (start us, length us, event | category | flops | bytes accessed | tf_op | source)
XLA Modules:
  0.0 29.8 jit_solution(2785257220422437208)
XLA Ops:
  0.6 28.5 %shard_map.102 = (f32[32,432]{1,0:T(8,128)S(1)}, f32[8,128]{1,0:T(8,128)S(1)}, f32[8,4,96]{2,1,0:T(4,128)S(1)}) custom-call(bf16[4,4,128,128]{3,2,1,0:T(8,128)(2,1)} %frames.1, bf16[3456,128]{1,0:T(8,128)(2,1)} %weight_in.1, f32[1,128]{1,0:T(1,128)} %bitcast.6, f32[6,128]{1,0:T(8,128)} %bitcast.5, s32[6]{0:T(128)} %levels_in.1, f32[8,4,96]{2,1,0:T(4,128)} %code_in.1, ...), custom_call_target="tpu_custom_call" | custom-call | tf_op jit(solution)/shard_map/pallas_call | solution.py:534
  29.1 0.6 %shard_map.103 = (f32[8,4,96]{2,1,0:T(4,128)}, f32[32,432]{1,0:T(8,128)}, f32[6,128]{1,0:T(8,128)}, f32[1,128]{1,0:T(1,128)}) custom-call(f32[8,4,96]{2,1,0:T(4,128)S(1)} %get-tuple-element.11.quant, f32[32,432]{1,0:T(8,128)S(1)} %get-tuple-element.12.wg, f32[8,128]{1,0:T(8,128)S(1)} %get-tuple-element.13.small), custom_call_target="tpu_custom_call" | custom-call | tf_op jit(solution)/shard_map/pallas_call | solution.py:582
